TPU v7x, 32 devices: a whole 2x2x4 slice. The times are simulated.
32 devices in a mesh: expert: 4 (over z), tensor: 8 (over y, x, core).
Axes of the slice: x: 2, y: 2, z: 4, core: 2. Of those that a mesh axis runs over, the one named last changes fastest.
Arguments:
- tokens: bfloat16 [1024, 4096], P(('expert', 'tensor')), may hold values from -6 to 6
- router: float32 [4096, 4], replicated, may hold values from -0.09375 to 0.09375
- choice_ids: int32 [1024, 2], P(('expert', 'tensor')), may hold values from 0 to 3, all different within a row; in each aligned block of 32 rows (0 to 31, 32 to 63, ...) at most 20 rows name the same one
- w_gate: bfloat16 [4, 4096, 14336], P('expert', None, 'tensor'), may hold values from -0.09375 to 0.09375
- w_up: bfloat16 [4, 4096, 14336], P('expert', None, 'tensor'), may hold values from -0.09375 to 0.09375
- w_down: bfloat16 [4, 14336, 4096], P('expert', 'tensor'), may hold values from -0.046875 to 0.046875
Outputs:
- mixed: bfloat16 [1024, 4096], P(('expert', 'tensor'))
Inputs may be any that keep to these rules, and one draw needn't show every extreme that they name: `choice_ids`: the 2 experts of a token differ. In each aligned block of 32 rows (the rows of one device) each expert is named by at most 20 rows, a bound that some block reaches.
All inputs are finite; a program needn't handle non-finite values.
Results may differ from a plain program's by a relative error of at most 0.015.
Values may be sent and summed in bfloat16 or wider, within the bound.
No kernel may reach another device: no remote copies, remote signals or barrier semaphores. Data moves between devices by JAX's collectives and lax.ppermute only.
A program may use at most 128 MiB of HBM per device.

v0:
```python
import jax
import jax.numpy as jnp
from jax import lax
from jax.sharding import PartitionSpec as P


def hidden_units(row_piece, weight_gate, weight_up):
    gate_proj = jnp.dot(row_piece, weight_gate, preferred_element_type=jnp.float32)
    up_proj = jnp.dot(row_piece, weight_up, preferred_element_type=jnp.float32)
    return (jax.nn.silu(gate_proj) * up_proj).astype(jnp.bfloat16)


def on_device(tokens, router, choice_ids, w_gate, w_up, w_down):
    tok_count, feat_width = tokens.shape
    top_count = choice_ids.shape[1]
    experts = lax.axis_size("expert")
    capacity = tok_count * top_count * 5 // (experts * 4)
    group_rows = experts * capacity
    weight_gate = w_gate[0]
    weight_up = w_up[0]
    weight_down = w_down[0]
    logits = jnp.dot(tokens.astype(jnp.float32), router, precision=lax.Precision.HIGHEST)
    picked = jnp.take_along_axis(logits, choice_ids, axis=1)
    gate_weights = jax.nn.softmax(picked, axis=1)
    flat_ids = choice_ids.reshape(-1)
    onehot = (flat_ids[:, None] == jnp.arange(experts, dtype=jnp.int32)[None, :]).astype(jnp.int32)
    slot_rank = jnp.cumsum(onehot, axis=0) - onehot
    slot_index = jnp.sum(slot_rank * onehot, axis=1)
    destination = flat_ids * capacity + slot_index
    dispatch_map = (
        jnp.arange(group_rows, dtype=jnp.int32)[:, None] == destination[None, :]
    ).astype(jnp.bfloat16)
    doubled = jnp.repeat(tokens, top_count, axis=0)
    buffer = jnp.dot(dispatch_map, doubled, preferred_element_type=jnp.float32).astype(jnp.bfloat16)
    arrived = lax.all_to_all(buffer, "expert", split_axis=0, concat_axis=0, tiled=True)
    hidden = hidden_units(
        lax.all_gather(arrived, "tensor", axis=0, tiled=True), weight_gate, weight_up
    )
    partial_value = jnp.dot(hidden, weight_down, preferred_element_type=jnp.float32)
    summed = lax.psum(partial_value.astype(jnp.bfloat16), "tensor").astype(jnp.float32)
    own_rows = lax.dynamic_slice_in_dim(
        summed, lax.axis_index("tensor") * group_rows, group_rows, 0
    )
    expert_out = own_rows.astype(jnp.bfloat16)
    returned = lax.all_to_all(expert_out, "expert", split_axis=0, concat_axis=0, tiled=True)
    gathered = jnp.dot(dispatch_map.T, returned, preferred_element_type=jnp.float32).reshape(
        tok_count, top_count, feat_width
    )
    result = jnp.sum(gathered * gate_weights[:, :, None], axis=1)
    return result.astype(jnp.bfloat16)


def solution(mesh):
    in_specs = (
        P(("expert", "tensor"), None),
        P(),
        P(("expert", "tensor"), None),
        P("expert", None, "tensor"),
        P("expert", None, "tensor"),
        P("expert", "tensor", None),
    )
    out_specs = P(("expert", "tensor"), None)
    return jax.shard_map(
        on_device, mesh=mesh, in_specs=in_specs, out_specs=out_specs, check_vma=False
    )
```

profile of v0, /device:TPU:0, one launch (start us, length us, event | category | flops | bytes accessed | tf_op | source)
XLA Modules:
  0.0 253.6 jit_solution(12875386895920183099)
XLA Ops:
  6.5 0.8 copy.26
  7.3 0.1 reshape.74
  7.5 0.1 reduce_window_sum.11
  7.6 0.2 select_reduce_fusion
  7.8 1.4 broadcast_in_dim.6
  9.2 0.2 reshape.75
  9.5 0.3 convolution_convert_fusion
  9.8 0.1 all_to_all.16
  9.9 26.3 %all_to_all.24 = bf16[4,20,4096]{2,1,0:T(8,128)(2,1)S(1)} all-to-all(bf16[4,20,4096]{2,1,0:T(8,128)(2,1)S(1)} %all_to_all.16), channel_id=1, replica_groups=mesh['expert'=4,'tensor'=8] {'expert'}, dimensions={0} | all-to-all | bytes 1310720 | tf_op jit(solution)/shard_map/all_to_all | solution.py:35
  36.2 1.0 all_to_all.18
  37.3 40.2 %all-gather.2.cloned.1.call-done = bf16[640,4096]{1,0:T(8,128)(2,1)} async-done(((bf16[80,4096]{1,0:T(8,128)(2,1)}), bf16[640,4096]{1,0:T(8,128)(2,1)}) %all-gather.2.cloned.1.call-update) | async-done | bytes 5242896 | tf_op jit(solution)/shard_map/all_gather | solution.py:37
  77.4 15.9 %fusion.4 = f32[640,1792]{1,0:T(8,128)} fusion(bf16[640,4096]{1,0:T(8,128)(2,1)} %all-gather.2.cloned.1.call-done, bf16[1,4096,1792]{2,1,0:T(8,128)(2,1)} %param.9), kind=kOutput, calls=%fused_computation.5 | convolution fusion | flops 9395240960 | bytes 24510464 | tf_op jit(solution)/shard_map/dot_general | solution.py:8
  93.3 33.1 %fusion.6 = bf16[640,4096]{1,0:T(8,128)(2,1)} fusion(bf16[1,1792,4096]{2,1,0:T(8,128)(2,1)} %param.11, f32[640,1792]{1,0:T(8,128)} %fusion.4, bf16[640,4096]{1,0:T(8,128)(2,1)} %all-gather.2.cloned.1.call-done, bf16[1,4096,1792]{2,1,0:T(8,128)(2,1)} %param.10), kind=kOutput, calls=%fused_computation.7 | convolution fusion | flops 18799984640 | bytes 44433408 | tf_op jit(solution)/shard_map/dot_general | solution.py:39
  126.5 0.6 copy-done.2
  127.2 0.1 reshape.77
  127.4 91.7 %all-reduce.2.cloned.1.call-done = bf16[640,4096]{1,0:T(8,128)(2,1)} async-done(((bf16[640,4096]{1,0:T(8,128)(2,1)}), bf16[640,4096]{1,0:T(8,128)(2,1)}) %all-reduce.2.cloned.1.call-update) | async-done | bytes 5242896 | tf_op jit(solution)/shard_map/psum | solution.py:40
  219.0 1.1 convert_convert_fusion
  220.1 1.0 all_to_all.19
  221.2 4.6 %all-to-all-start.1 = ((bf16[4,20,4096]{2,1,0:T(8,128)(2,1)}), bf16[4,20,4096]{2,1,0:T(8,128)(2,1)S(1)}, u32[]{:S(2)}, u32[]{:S(2)}) async-start(bf16[4,20,4096]{2,1,0:T(8,128)(2,1)} %all_to_all.19), calls=%async_computation.1 | async-start | bytes 1572864 | tf_op jit(solution)/shard_map/all_to_all | solution.py:45
  225.8 0.3 fusion.22
  226.1 0.9 gather_fusion
  227.3 18.3 %all-to-all-done.1 = bf16[4,20,4096]{2,1,0:T(8,128)(2,1)S(1)} async-done(((bf16[4,20,4096]{2,1,0:T(8,128)(2,1)}), bf16[4,20,4096]{2,1,0:T(8,128)(2,1)S(1)}, u32[]{:S(2)}, u32[]{:S(2)}) %all-to-all-start.1) | async-done | bytes 655392 | tf_op jit(solution)/shard_map/all_to_all | solution.py:45
  245.6 0.1 reshape.88
  245.8 1.0 fusion.14
  (24 shorter events, 0.6 us)
Async XLA Ops:
  6.5 219.2 %copy-start = (f32[4096,4]{0,1:T(4,128)S(1)}, f32[4096,4]{0,1:T(4,128)}, u32[]{:S(2)}) copy-start(f32[4096,4]{0,1:T(4,128)} %param.7) | copy-start | bytes 196612
  6.5 70.9 %all-gather.2.cloned.1.call-start = ((), (), s32[]{:S(2)}) async-start(), calls=%async_computation.2 | async-start | bytes 5898240 | tf_op jit(solution)/shard_map/all_gather | solution.py:37
  7.8 2.0 copy-start.3
  37.2 181.8 %all-reduce.2.cloned.1.call-start = ((), (), s32[]{:S(2)}) async-start(), calls=%async_computation.3 | async-start | bytes 10485760 | tf_op jit(solution)/shard_map/psum | solution.py:40
  126.5 0.7 copy-start.2
  126.5 99.3 %copy-start.1 = (bf16[32,4096]{1,0:T(8,128)(2,1)S(1)}, bf16[32,4096]{1,0:T(8,128)(2,1)}, u32[]{:S(2)}) copy-start(bf16[32,4096]{1,0:T(8,128)(2,1)} %param.6) | copy-start | bytes 786436
  221.2 24.4 %all-to-all-start.1 = ((bf16[4,20,4096]{2,1,0:T(8,128)(2,1)}), bf16[4,20,4096]{2,1,0:T(8,128)(2,1)S(1)}, u32[]{:S(2)}, u32[]{:S(2)}) async-start(bf16[4,20,4096]{2,1,0:T(8,128)(2,1)} %all_to_all.19), calls=%async_computation.1 | async-start | bytes 1572864 | tf_op jit(solution)/shard_map/all_to_all | solution.py:45
  226.1 1.1 copy-start.4
Sparse Core Ops, SparseCore 0:
  37.3 40.0 all-gather.1
  126.6 92.3 all-reduce.1
where the time goes:
time: 254 us
  waiting for transfers between devices  150 us (59%)
  matrix products  50.6 us (20%)
  blocking collectives  26.3 us (10%)
  between operations  13.5 us (5%)
  local copies, waits for them, and re-layouts  6.75 us (3%)
  starting transfers between devices  4.64 us (2%)
    psum x1, waiting for transfers between devices, on_device(): lax.psum(partial_value.astype(jnp.bfloat16), 'tensor').astype(jnp.float32)  91.7 us
    all_gather x1, waiting for transfers between devices, on_device(): lax.all_gather(arrived, 'tensor', axis=0, tiled=True)  40.2 us
    dot_general x1, matrix products, on_device(): jnp.dot(hidden, weight_down, preferred_element_type=jnp.float32)  33.1 us
    all_to_all x1, blocking collectives, on_device(): lax.all_to_all(buffer, 'expert', split_axis=0, concat_axis=0, tiled=True)  26.3 us
    all_to_all x1, waiting for transfers between devices, on_device(): lax.all_to_all(expert_out, 'expert', split_axis=0, concat_axis=0, tiled=T...  18.3 us
    dot_general x1, matrix products, hidden_units(): jnp.dot(row_piece, weight_gate, preferred_element_type=jnp.float32)  15.9 us
  transfers between devices with their start and end apart: 3, of which 3 were waited for; matrix products, arithmetic and copies ran while one was open for 1% of the time, Pallas kernels for 0%

commit v1 on v0

v1 whole, which is shorter than its diff:
```python
import jax
import jax.numpy as jnp
from jax import lax
from jax.sharding import PartitionSpec as P

CHUNKS = 2


def swap(value, axis, size, bit):
    return lax.ppermute(value, axis, [(i, i ^ bit) for i in range(size)])


def shift(value, axis, size, step):
    return lax.ppermute(value, axis, [(i, (i + step) % size) for i in range(size)])


def lane_orders(size):
    bits = [1 << b for b in range(size.bit_length() - 1)]
    return [bits[1:], bits[1:][::-1]], bits[0]


def gather_lane(piece, size, order):
    pieces = {0: piece}
    rows = piece.shape[0]
    for bit in order:
        keys = sorted(pieces)
        sent = jnp.concatenate([pieces[key] for key in keys], 0) if len(keys) > 1 else pieces[keys[0]]
        came = swap(sent, "tensor", size, bit)
        for place, key in enumerate(keys):
            pieces[key ^ bit] = came[place * rows : (place + 1) * rows]
    return jnp.concatenate([pieces[key] for key in sorted(pieces)], 0)


def scatter_lane(pieces, size, order):
    for bit in reversed(order):
        kept = sorted(key for key in pieces if not key & bit)
        rows = pieces[kept[0]].shape[0]
        sent = jnp.concatenate([pieces[key ^ bit] for key in kept], 0)
        came = swap(sent, "tensor", size, bit)
        pieces = {
            key: (
                pieces[key].astype(jnp.float32)
                + came[place * rows : (place + 1) * rows].astype(jnp.float32)
            ).astype(jnp.bfloat16)
            for place, key in enumerate(kept)
        }
    return pieces[0]


def gather_rows(rows, size):
    orders, last = lane_orders(size)
    width = rows.shape[1] // len(orders)
    lanes = [
        gather_lane(rows[:, lane * width : (lane + 1) * width], size, order)
        for lane, order in enumerate(orders)
    ]
    mine = jnp.concatenate(lanes, 1)
    return jnp.concatenate([mine, swap(mine, "tensor", size, last)], 0)


def scatter_rows(partial_value, size):
    orders, last = lane_orders(size)
    half = partial_value.shape[0] // 2
    came = swap(partial_value[half:], "tensor", size, last)
    total = (partial_value[:half].astype(jnp.float32) + came.astype(jnp.float32)).astype(
        jnp.bfloat16
    )
    width = total.shape[1] // len(orders)
    count = size // 2
    rows = half // count
    lanes = []
    for lane, order in enumerate(orders):
        columns = total[:, lane * width : (lane + 1) * width]
        pieces = {
            2 * place: columns[place * rows : (place + 1) * rows] for place in range(count)
        }
        lanes.append(scatter_lane(pieces, size, order))
    return jnp.concatenate(lanes, 1)


def expert_rows(rows, weight_gate, weight_up, weight_down):
    gate_proj = jnp.dot(rows, weight_gate, preferred_element_type=jnp.float32)
    up_proj = jnp.dot(rows, weight_up, preferred_element_type=jnp.float32)
    hidden = (jax.nn.silu(gate_proj) * up_proj).astype(jnp.bfloat16)
    return jnp.dot(hidden, weight_down, preferred_element_type=jnp.float32).astype(jnp.bfloat16)


def on_device(tokens, router, choice_ids, w_gate, w_up, w_down):
    tok_count = tokens.shape[0]
    top_count = choice_ids.shape[1]
    experts = lax.axis_size("expert")
    size = lax.axis_size("tensor")
    capacity = tok_count * top_count * 5 // (experts * 4)
    group_rows = experts * capacity
    plane = lax.axis_index("expert")

    flat_ids = choice_ids.reshape(-1)
    onehot = (flat_ids[:, None] == jnp.arange(experts, dtype=jnp.int32)[None, :]).astype(jnp.int32)
    slot_rank = jnp.cumsum(onehot, axis=0) - onehot
    slot_index = jnp.sum(slot_rank * onehot, axis=1)
    relative = jnp.mod(flat_ids - plane, experts)
    destination = (relative * capacity + slot_index).reshape(tok_count, top_count)
    named = jnp.arange(group_rows, dtype=jnp.int32)[:, None, None] == destination[None]
    dispatch_map = jnp.any(named, axis=2).astype(jnp.bfloat16)
    buffer = jnp.dot(dispatch_map, tokens, preferred_element_type=jnp.float32).astype(jnp.bfloat16)

    arrived = [
        buffer[:capacity]
        if step == 0
        else shift(buffer[step * capacity : (step + 1) * capacity], "expert", experts, step)
        for step in range(experts)
    ]
    per_chunk = experts // CHUNKS
    returned = []
    for chunk in range(CHUNKS):
        rows = jnp.concatenate(arrived[chunk * per_chunk : (chunk + 1) * per_chunk], 0)
        partial_value = expert_rows(gather_rows(rows, size), w_gate[0], w_up[0], w_down[0])
        own = scatter_rows(partial_value, size)
        for place in range(per_chunk):
            step = chunk * per_chunk + place
            piece = own[place * capacity : (place + 1) * capacity]
            returned.append(piece if step == 0 else shift(piece, "expert", experts, -step))
    returned = jnp.concatenate(returned, 0)

    logits = jnp.dot(tokens.astype(jnp.float32), router, precision=lax.Precision.HIGHEST)
    picked = jnp.take_along_axis(logits, choice_ids, axis=1)
    gate_weights = jax.nn.softmax(picked, axis=1)
    result = 0.0
    for k in range(top_count):
        chosen = (
            destination[:, k][:, None] == jnp.arange(group_rows, dtype=jnp.int32)[None, :]
        ).astype(jnp.bfloat16)
        taken = jnp.dot(chosen, returned, preferred_element_type=jnp.float32)
        result = result + taken * gate_weights[:, k][:, None]
    return result.astype(jnp.bfloat16)


def solution(mesh):
    in_specs = (
        P(("expert", "tensor"), None),
        P(),
        P(("expert", "tensor"), None),
        P("expert", None, "tensor"),
        P("expert", None, "tensor"),
        P("expert", "tensor", None),
    )
    out_specs = P(("expert", "tensor"), None)
    return jax.shard_map(
        on_device, mesh=mesh, in_specs=in_specs, out_specs=out_specs, check_vma=False
    )
```

time: 254 us -> 162 us (0.64)
  waiting for transfers between devices: 150 us -> 55.2 us
  starting transfers between devices: 4.64 us -> 36.4 us
  blocking collectives: 26.3 us -> 0 us
  between operations: 13.5 us -> 0.42 us
  matrix products: 50.6 us -> 62.2 us
  local copies, waits for them, and re-layouts: 6.75 us -> 3.38 us
    psum x1 -> x0, waiting for transfers between devices: 91.7 us -> none  [on_device(): lax.psum(partial_value.astype(jnp.bfloat16), 'tensor').astype(jnp.float32)]
    ppermute x0 -> x26, waiting for transfers between devices: none -> 55.2 us  [the longest x20 39.2 us: swap(): return lax.ppermute(value, axis, [(i, i ^ bit) for i in range(size)])]
    all_gather x1 -> x0, waiting for transfers between devices: 40.2 us -> none  [on_device(): lax.all_gather(arrived, 'tensor', axis=0, tiled=True)]
    ppermute x0 -> x26, starting transfers between devices: none -> 36.4 us  [the longest x20 20.6 us: swap(): return lax.ppermute(value, axis, [(i, i ^ bit) for i in range(size)])]
    all_to_all x1 -> x0, blocking collectives: 26.3 us -> none  [on_device(): lax.all_to_all(buffer, 'expert', split_axis=0, concat_axis=0, tiled=True)]
    all_to_all x1 -> x0, waiting for transfers between devices: 18.3 us -> none  [on_device(): lax.all_to_all(expert_out, 'expert', split_axis=0, concat_axis=0, tiled=T...]
    dot_general x4 -> x9, matrix products: 50.3 us -> 61.9 us  [the longest x2 22 us: expert_rows(): jnp.dot(hidden, weight_down, preferred_element_type=jnp.float32)]
    all_to_all x1 -> x0, starting transfers between devices: 4.6 us -> none  [on_device(): lax.all_to_all(expert_out, 'expert', split_axis=0, concat_axis=0, tiled=T...]
  transfers between devices with their start and end apart: 3 -> 26, of which waited for: 3 -> 15; matrix products, arithmetic and copies ran while one was open for 1% -> 40% of each run, Pallas kernels for 0% -> 0%
where the time goes in v1:
time: 162 us
  matrix products  62.2 us (38%)
  waiting for transfers between devices  55.2 us (34%)
  starting transfers between devices  36.4 us (22%)
  other arithmetic  4.04 us (2%)
  local copies, waits for them, and re-layouts  3.38 us (2%)
    ppermute x20, waiting for transfers between devices, swap(): return lax.ppermute(value, axis, [(i, i ^ bit) for i in range(size)])  39.2 us
    dot_general x2, matrix products, expert_rows(): jnp.dot(hidden, weight_down, preferred_element_type=jnp.float32)  22 us
    dot_general x2, matrix products, expert_rows(): gate_proj = jnp.dot(rows, weight_gate, preferred_element_type=jnp.float32)  21.9 us
    ppermute x20, starting transfers between devices, swap(): return lax.ppermute(value, axis, [(i, i ^ bit) for i in range(size)])  20.6 us
    dot_general x2, matrix products, expert_rows(): up_proj = jnp.dot(rows, weight_up, preferred_element_type=jnp.float32)  16.4 us
    ppermute x6, waiting for transfers between devices, shift(): lax.ppermute(value, axis, [(i, (i + step) % size) for i in range(size)])  16 us
    ppermute x6, starting transfers between devices, shift(): lax.ppermute(value, axis, [(i, (i + step) % size) for i in range(size)])  15.9 us
  transfers between devices with their start and end apart: 26, of which 15 were waited for; matrix products, arithmetic and copies ran while one was open for 40% of the time, Pallas kernels for 0%

profile of v1, /device:TPU:0, one launch (start us, length us, event | category | flops | bytes accessed | tf_op | source)
XLA Modules:
  0.0 161.7 jit_solution(7405311585623538856)
XLA Ops:
  3.6 4.1 %collective-permute-start.12 = (bf16[20,4096]{1,0:T(8,128)(2,1)S(1)}, bf16[20,4096]{1,0:T(8,128)(2,1)S(1)}, u32[]{:S(2)}, u32[]{:S(2)}) collective-permute-start(bf16[20,4096]{1,0:T(8,128)(2,1)S(1)} %get-tuple-element.21), channel_id=1, source_target_pairs={{0,16},{8,24},{16,0},{24,8},{1,17},{9,25},{17,1},{25,9},{2,18},{10... | collective-permute-start | bytes 491528 | tf_op jit(solution)/shard_map/ppermute | solution.py:14
  11.7 6.9 %collective-permute-done.12 = bf16[20,4096]{1,0:T(8,128)(2,1)S(1)} collective-permute-done((bf16[20,4096]{1,0:T(8,128)(2,1)S(1)}, bf16[20,4096]{1,0:T(8,128)(2,1)S(1)}, u32[]{:S(2)}, u32[]{:S(2)}) %collective-permute-start.12) | collective-permute-done | bytes 163872 | tf_op jit(solution)/shard_map/ppermute | solution.py:14
  18.7 2.1 %collective-permute-start.16 = (bf16[40,2048]{1,0:T(8,128)(2,1)S(1)}, bf16[40,2048]{1,0:T(8,128)(2,1)S(1)}, u32[]{:S(2)}, u32[]{:S(2)}) collective-permute-start(bf16[40,2048]{1,0:T(8,128)(2,1)S(1)} %get-tuple-element.26), channel_id=1, source_target_pairs={{0,4},{1,5},{2,6},{3,7},{4,0},{5,1},{6,2},{7,3},{8,12},{9,13},{10,... | collective-permute-start | bytes 491528 | tf_op jit(solution)/shard_map/ppermute | solution.py:10
  22.4 1.6 collective-permute-start.3
  28.7 2.3 %collective-permute-start.4 = (bf16[80,2048]{1,0:T(8,128)(2,1)S(1)}, bf16[80,2048]{1,0:T(8,128)(2,1)S(1)}, u32[]{:S(2)}, u32[]{:S(2)}) collective-permute-start(bf16[80,2048]{1,0:T(8,128)(2,1)S(1)} %pad_maximum_fusion.4), channel_id=1, source_target_pairs={{0,2},{1,3},{2,0},{3,1},{4,6},{5,7},{6,4},{7,5},{8,10},{9,11},{10,... | collective-permute-start | bytes 983048 | tf_op jit(solution)/shard_map/ppermute | solution.py:10
  31.0 7.1 %collective-permute-done.17 = bf16[80,2048]{1,0:T(8,128)(2,1)S(1)} collective-permute-done((bf16[80,2048]{1,0:T(8,128)(2,1)S(1)}, bf16[80,2048]{1,0:T(8,128)(2,1)S(1)}, u32[]{:S(2)}, u32[]{:S(2)}) %collective-permute-start.17) | collective-permute-done | bytes 327712 | tf_op jit(solution)/shard_map/ppermute | solution.py:10
  39.0 4.7 %collective-permute-done.4 = bf16[80,2048]{1,0:T(8,128)(2,1)S(1)} collective-permute-done((bf16[80,2048]{1,0:T(8,128)(2,1)S(1)}, bf16[80,2048]{1,0:T(8,128)(2,1)S(1)}, u32[]{:S(2)}, u32[]{:S(2)}) %collective-permute-start.4) | collective-permute-done | bytes 327712 | tf_op jit(solution)/shard_map/ppermute | solution.py:10
  43.7 4.9 %collective-permute-done.2 = bf16[80,2048]{1,0:T(8,128)(2,1)S(1)} collective-permute-done((bf16[80,2048]{1,0:T(8,128)(2,1)S(1)}, bf16[80,2048]{1,0:T(8,128)(2,1)S(1)}, u32[]{:S(2)}, u32[]{:S(2)}) %collective-permute-start.2) | collective-permute-done | bytes 327712 | tf_op jit(solution)/shard_map/ppermute | solution.py:10
  48.8 10.1 %fusion.4 = f32[320,1792]{1,0:T(8,128)S(1)} fusion(bf16[1,4096,1792]{2,1,0:T(8,128)(2,1)} %param.10, bf16[160,4096]{1,0:T(8,128)(2,1)S(1)} %collective-permute-done.18, bf16[40,2048]{1,0:T(8,128)(2,1)S(1)} %get-tuple-element.34, bf16[40,2048]{1,0:T(8,128)(2,1)S(1)} %collective-permute-done.16, bf16[40,2048]{1,0:T(8,128)(2,1)S(1)} %get-tuple-element.33, ...), kind=kOutput, calls=%fused_computation.5 | convolution fusion | flops 4718592000 | bytes 19595264 | tf_op jit(solution)/shard_map/dot_general | solution.py:83
  58.9 11.6 %fusion.8 = f32[320,1792]{1,0:T(8,128)} fusion(bf16[1,4096,1792]{2,1,0:T(8,128)(2,1)} %param.9, bf16[160,4096]{1,0:T(8,128)(2,1)S(1)} %collective-permute-done.18, bf16[40,2048]{1,0:T(8,128)(2,1)S(1)} %get-tuple-element.34, bf16[40,2048]{1,0:T(8,128)(2,1)S(1)} %collective-permute-done.16, bf16[40,2048]{1,0:T(8,128)(2,1)S(1)} %get-tuple-element.33, ...), kind=kOutput, calls=%fused_computation.9 | convolution fusion | flops 4718592000 | bytes 19595264 | tf_op jit(solution)/shard_map/dot_general | solution.py:82
  70.6 11.2 %fusion.15 = bf16[320,4096]{1,0:T(8,128)(2,1)S(1)} fusion(bf16[1,1792,4096]{2,1,0:T(8,128)(2,1)} %param.11, f32[320,1792]{1,0:T(8,128)S(1)} %fusion.4, f32[320,1792]{1,0:T(8,128)} %fusion.8), kind=kOutput, calls=%fused_computation.14 | convolution fusion | flops 4702371840 | bytes 21889024 | tf_op jit(solution)/shard_map/dot_general | solution.py:85
  82.5 6.4 %fusion.6 = f32[320,1792]{1,0:T(8,128)} fusion(bf16[1,4096,1792]{2,1,0:T(8,128)(2,1)S(1)} %bitcast.28, bf16[160,4096]{1,0:T(8,128)(2,1)S(1)} %collective-permute-done.5, bf16[40,2048]{1,0:T(8,128)(2,1)S(1)} %get-tuple-element.30, bf16[40,2048]{1,0:T(8,128)(2,1)S(1)} %collective-permute-done.3, bf16[40,2048]{1,0:T(8,128)(2,1)S(1)} %get-tuple-element.29, ...), kind=kOutput, calls=%fused_computation.7 | convolution fusion | flops 4718592000 | bytes 19595264 | tf_op jit(solution)/shard_map/dot_general | solution.py:83
  88.9 10.2 %fusion.10 = f32[320,1792]{1,0:T(8,128)S(1)} fusion(bf16[1,4096,1792]{2,1,0:T(8,128)(2,1)} %param.9, bf16[160,4096]{1,0:T(8,128)(2,1)S(1)} %collective-permute-done.5, bf16[40,2048]{1,0:T(8,128)(2,1)S(1)} %get-tuple-element.30, bf16[40,2048]{1,0:T(8,128)(2,1)S(1)} %collective-permute-done.3, bf16[40,2048]{1,0:T(8,128)(2,1)S(1)} %get-tuple-element.29, ...), kind=kOutput, calls=%fused_computation.11 | convolution fusion | flops 4718592000 | bytes 19595264 | tf_op jit(solution)/shard_map/dot_general | solution.py:82
  99.1 10.7 %fusion.12 = bf16[320,4096]{1,0:T(8,128)(2,1)S(1)} fusion(bf16[1,1792,4096]{2,1,0:T(8,128)(2,1)} %param.11, f32[320,1792]{1,0:T(8,128)S(1)} %copy-done.3, f32[320,1792]{1,0:T(8,128)S(1)} %fusion.10), kind=kOutput, calls=%fused_computation.13 | convolution fusion | flops 4702371840 | bytes 21889024 | tf_op jit(solution)/shard_map/dot_general | solution.py:85
  111.1 1.9 %collective-permute-done.6 = bf16[160,4096]{1,0:T(8,128)(2,1)S(1)} collective-permute-done((bf16[160,4096]{1,0:T(8,128)(2,1)S(1)}, bf16[160,4096]{1,0:T(8,128)(2,1)S(1)}, u32[]{:S(2)}, u32[]{:S(2)}) %collective-permute-start.6) | collective-permute-done | bytes 1310752 | tf_op jit(solution)/shard_map/ppermute | solution.py:10
  116.2 4.9 %collective-permute-done.20 = bf16[80,2048]{1,0:T(8,128)(2,1)S(1)} collective-permute-done((bf16[80,2048]{1,0:T(8,128)(2,1)S(1)}, bf16[80,2048]{1,0:T(8,128)(2,1)S(1)}, u32[]{:S(2)}, u32[]{:S(2)}) %collective-permute-start.20) | collective-permute-done | bytes 327712 | tf_op jit(solution)/shard_map/ppermute | solution.py:10
  122.7 5.0 %collective-permute-done.7 = bf16[80,2048]{1,0:T(8,128)(2,1)S(1)} collective-permute-done((bf16[80,2048]{1,0:T(8,128)(2,1)S(1)}, bf16[80,2048]{1,0:T(8,128)(2,1)S(1)}, u32[]{:S(2)}, u32[]{:S(2)}) %collective-permute-start.7) | collective-permute-done | bytes 327712 | tf_op jit(solution)/shard_map/ppermute | solution.py:10
  129.3 5.5 %collective-permute-done.21 = bf16[40,2048]{1,0:T(8,128)(2,1)S(1)} collective-permute-done((bf16[40,2048]{1,0:T(8,128)(2,1)S(1)}, bf16[40,2048]{1,0:T(8,128)(2,1)S(1)}, u32[]{:S(2)}, u32[]{:S(2)}) %collective-permute-start.21) | collective-permute-done | bytes 163872 | tf_op jit(solution)/shard_map/ppermute | solution.py:10
  135.4 2.0 %collective-permute-done.8 = bf16[40,2048]{1,0:T(8,128)(2,1)S(1)} collective-permute-done((bf16[40,2048]{1,0:T(8,128)(2,1)S(1)}, bf16[40,2048]{1,0:T(8,128)(2,1)S(1)}, u32[]{:S(2)}, u32[]{:S(2)}) %collective-permute-start.8) | collective-permute-done | bytes 163872 | tf_op jit(solution)/shard_map/ppermute | solution.py:10
  138.1 2.9 %collective-permute-done.23 = bf16[40,2048]{1,0:T(8,128)(2,1)S(1)} collective-permute-done((bf16[40,2048]{1,0:T(8,128)(2,1)S(1)}, bf16[40,2048]{1,0:T(8,128)(2,1)S(1)}, u32[]{:S(2)}, u32[]{:S(2)}) %collective-permute-start.23) | collective-permute-done | bytes 163872 | tf_op jit(solution)/shard_map/ppermute | solution.py:10
  141.1 7.2 %collective-permute-start.25 = (bf16[20,4096]{1,0:T(8,128)(2,1)S(1)}, bf16[20,4096]{1,0:T(8,128)(2,1)S(1)}, u32[]{:S(2)}, u32[]{:S(2)}) collective-permute-start(bf16[20,4096]{1,0:T(8,128)(2,1)S(1)} %get-tuple-element.32), channel_id=1, source_target_pairs={{0,8},{8,16},{16,24},{24,0},{1,9},{9,17},{17,25},{25,1},{2,10},{10... | collective-permute-start | bytes 491528 | tf_op jit(solution)/shard_map/ppermute | solution.py:14
  148.5 2.5 %collective-permute-start.11 = (bf16[20,4096]{1,0:T(8,128)(2,1)S(1)}, bf16[20,4096]{1,0:T(8,128)(2,1)S(1)}, u32[]{:S(2)}, u32[]{:S(2)}) collective-permute-start(bf16[20,4096]{1,0:T(8,128)(2,1)S(1)} %get-tuple-element.28), channel_id=1, source_target_pairs={{0,24},{8,0},{16,8},{24,16},{1,25},{9,1},{17,9},{25,17},{2,26},{10... | collective-permute-start | bytes 491528 | tf_op jit(solution)/shard_map/ppermute | solution.py:14
  151.3 2.1 %collective-permute-done.25 = bf16[20,4096]{1,0:T(8,128)(2,1)S(1)} collective-permute-done((bf16[20,4096]{1,0:T(8,128)(2,1)S(1)}, bf16[20,4096]{1,0:T(8,128)(2,1)S(1)}, u32[]{:S(2)}, u32[]{:S(2)}) %collective-permute-start.25) | collective-permute-done | bytes 163872 | tf_op jit(solution)/shard_map/ppermute | solution.py:14
  153.4 5.8 %collective-permute-done.24 = bf16[20,4096]{1,0:T(8,128)(2,1)S(1)} collective-permute-done((bf16[20,4096]{1,0:T(8,128)(2,1)S(1)}, bf16[20,4096]{1,0:T(8,128)(2,1)S(1)}, u32[]{:S(2)}, u32[]{:S(2)}) %collective-permute-start.24) | collective-permute-done | bytes 163872 | tf_op jit(solution)/shard_map/ppermute | solution.py:14
  (108 shorter events, 27.6 us)
Async XLA Ops:
  3.6 15.0 %collective-permute-start.12 = (bf16[20,4096]{1,0:T(8,128)(2,1)S(1)}, bf16[20,4096]{1,0:T(8,128)(2,1)S(1)}, u32[]{:S(2)}, u32[]{:S(2)}) collective-permute-start(bf16[20,4096]{1,0:T(8,128)(2,1)S(1)} %get-tuple-element.21), channel_id=1, source_target_pairs={{0,16},{8,24},{16,0},{24,8},{1,17},{9,25},{17,1},{25,9},{2,18},{10... | collective-permute-start | bytes 491528 | tf_op jit(solution)/shard_map/ppermute | solution.py:14
  7.8 10.9 %collective-permute-start.13 = (bf16[20,4096]{1,0:T(8,128)(2,1)S(1)}, bf16[20,4096]{1,0:T(8,128)(2,1)S(1)}, u32[]{:S(2)}, u32[]{:S(2)}) collective-permute-start(bf16[20,4096]{1,0:T(8,128)(2,1)S(1)} %get-tuple-element.20), channel_id=1, source_target_pairs={{0,24},{8,0},{16,8},{24,16},{1,25},{9,1},{17,9},{25,17},{2,26},{10... | collective-permute-start | bytes 491528 | tf_op jit(solution)/shard_map/ppermute | solution.py:14
  9.1 13.2 %collective-permute-start = (bf16[20,4096]{1,0:T(8,128)(2,1)S(1)}, bf16[20,4096]{1,0:T(8,128)(2,1)S(1)}, u32[]{:S(2)}, u32[]{:S(2)}) collective-permute-start(bf16[20,4096]{1,0:T(8,128)(2,1)S(1)} %get-tuple-element.22), channel_id=1, source_target_pairs={{0,8},{8,16},{16,24},{24,0},{1,9},{9,17},{17,25},{25,1},{2,10},{10... | collective-permute-start | bytes 491528 | tf_op jit(solution)/shard_map/ppermute | solution.py:14
  18.7 6.7 %collective-permute-start.16 = (bf16[40,2048]{1,0:T(8,128)(2,1)S(1)}, bf16[40,2048]{1,0:T(8,128)(2,1)S(1)}, u32[]{:S(2)}, u32[]{:S(2)}) collective-permute-start(bf16[40,2048]{1,0:T(8,128)(2,1)S(1)} %get-tuple-element.26), channel_id=1, source_target_pairs={{0,4},{1,5},{2,6},{3,7},{4,0},{5,1},{6,2},{7,3},{8,12},{9,13},{10,... | collective-permute-start | bytes 491528 | tf_op jit(solution)/shard_map/ppermute | solution.py:10
  20.8 6.2 %collective-permute-start.14 = (bf16[40,2048]{1,0:T(8,128)(2,1)S(1)}, bf16[40,2048]{1,0:T(8,128)(2,1)S(1)}, u32[]{:S(2)}, u32[]{:S(2)}) collective-permute-start(bf16[40,2048]{1,0:T(8,128)(2,1)S(1)} %get-tuple-element.25), channel_id=1, source_target_pairs={{0,2},{1,3},{2,0},{3,1},{4,6},{5,7},{6,4},{7,5},{8,10},{9,11},{10,... | collective-permute-start | bytes 491528 | tf_op jit(solution)/shard_map/ppermute | solution.py:10
  22.4 6.3 %collective-permute-start.3 = (bf16[40,2048]{1,0:T(8,128)(2,1)S(1)}, bf16[40,2048]{1,0:T(8,128)(2,1)S(1)}, u32[]{:S(2)}, u32[]{:S(2)}) collective-permute-start(bf16[40,2048]{1,0:T(8,128)(2,1)S(1)} %get-tuple-element.24), channel_id=1, source_target_pairs={{0,4},{1,5},{2,6},{3,7},{4,0},{5,1},{6,2},{7,3},{8,12},{9,13},{10,... | collective-permute-start | bytes 491528 | tf_op jit(solution)/shard_map/ppermute | solution.py:10
  24.0 14.4 %collective-permute-start.1 = (bf16[40,2048]{1,0:T(8,128)(2,1)S(1)}, bf16[40,2048]{1,0:T(8,128)(2,1)S(1)}, u32[]{:S(2)}, u32[]{:S(2)}) collective-permute-start(bf16[40,2048]{1,0:T(8,128)(2,1)S(1)} %get-tuple-element.23), channel_id=1, source_target_pairs={{0,2},{1,3},{2,0},{3,1},{4,6},{5,7},{6,4},{7,5},{8,10},{9,11},{10,... | collective-permute-start | bytes 491528 | tf_op jit(solution)/shard_map/ppermute | solution.py:10
  25.5 12.6 %collective-permute-start.17 = (bf16[80,2048]{1,0:T(8,128)(2,1)S(1)}, bf16[80,2048]{1,0:T(8,128)(2,1)S(1)}, u32[]{:S(2)}, u32[]{:S(2)}) collective-permute-start(bf16[80,2048]{1,0:T(8,128)(2,1)S(1)} %pad_maximum_fusion.7), channel_id=1, source_target_pairs={{0,2},{1,3},{2,0},{3,1},{4,6},{5,7},{6,4},{7,5},{8,10},{9,11},{10,... | collective-permute-start | bytes 983048 | tf_op jit(solution)/shard_map/ppermute | solution.py:10
  27.1 11.0 %collective-permute-start.15 = (bf16[80,2048]{1,0:T(8,128)(2,1)S(1)}, bf16[80,2048]{1,0:T(8,128)(2,1)S(1)}, u32[]{:S(2)}, u32[]{:S(2)}) collective-permute-start(bf16[80,2048]{1,0:T(8,128)(2,1)S(1)} %pad_maximum_fusion.6), channel_id=1, source_target_pairs={{0,4},{1,5},{2,6},{3,7},{4,0},{5,1},{6,2},{7,3},{8,12},{9,13},{10,... | collective-permute-start | bytes 983048 | tf_op jit(solution)/shard_map/ppermute | solution.py:10
  28.7 15.0 %collective-permute-start.4 = (bf16[80,2048]{1,0:T(8,128)(2,1)S(1)}, bf16[80,2048]{1,0:T(8,128)(2,1)S(1)}, u32[]{:S(2)}, u32[]{:S(2)}) collective-permute-start(bf16[80,2048]{1,0:T(8,128)(2,1)S(1)} %pad_maximum_fusion.4), channel_id=1, source_target_pairs={{0,2},{1,3},{2,0},{3,1},{4,6},{5,7},{6,4},{7,5},{8,10},{9,11},{10,... | collective-permute-start | bytes 983048 | tf_op jit(solution)/shard_map/ppermute | solution.py:10
  38.2 10.6 %collective-permute-start.18 = (bf16[160,4096]{1,0:T(8,128)(2,1)S(1)}, bf16[160,4096]{1,0:T(8,128)(2,1)S(1)}, u32[]{:S(2)}, u32[]{:S(2)}) collective-permute-start(bf16[160,4096]{1,0:T(8,128)(2,1)S(1)} %maximum_maximum_fusion.1), channel_id=1, source_target_pairs={{0,1},{1,0},{2,3},{3,2},{4,5},{5,4},{6,7},{7,6},{8,9},{9,8},{10,11... | collective-permute-start | bytes 3932168 | tf_op jit(solution)/shard_map/ppermute | solution.py:10
  38.4 10.2 %collective-permute-start.2 = (bf16[80,2048]{1,0:T(8,128)(2,1)S(1)}, bf16[80,2048]{1,0:T(8,128)(2,1)S(1)}, u32[]{:S(2)}, u32[]{:S(2)}) collective-permute-start(bf16[80,2048]{1,0:T(8,128)(2,1)S(1)} %pad_maximum_fusion.3), channel_id=1, source_target_pairs={{0,4},{1,5},{2,6},{3,7},{4,0},{5,1},{6,2},{7,3},{8,12},{9,13},{10,... | collective-permute-start | bytes 983048 | tf_op jit(solution)/shard_map/ppermute | solution.py:10
  48.7 33.8 %collective-permute-start.5 = (bf16[160,4096]{1,0:T(8,128)(2,1)S(1)}, bf16[160,4096]{1,0:T(8,128)(2,1)S(1)}, u32[]{:S(2)}, u32[]{:S(2)}) collective-permute-start(bf16[160,4096]{1,0:T(8,128)(2,1)S(1)} %maximum_maximum_fusion), channel_id=1, source_target_pairs={{0,1},{1,0},{2,3},{3,2},{4,5},{5,4},{6,7},{7,6},{8,9},{9,8},{10,11... | collective-permute-start | bytes 3932168 | tf_op jit(solution)/shard_map/ppermute | solution.py:10
  81.9 28.1 %collective-permute-start.19 = (bf16[160,4096]{1,0:T(8,128)(2,1)S(1)}, bf16[160,4096]{1,0:T(8,128)(2,1)S(1)}, u32[]{:S(2)}, u32[]{:S(2)}) collective-permute-start(bf16[160,4096]{1,0:T(8,128)(2,1)S(1)} %slice.238), channel_id=1, source_target_pairs={{0,1},{1,0},{2,3},{3,2},{4,5},{5,4},{6,7},{7,6},{8,9},{9,8},{10,11... | collective-permute-start | bytes 3932168 | tf_op jit(solution)/shard_map/ppermute | solution.py:10
  110.5 10.6 %collective-permute-start.20 = (bf16[80,2048]{1,0:T(8,128)(2,1)S(1)}, bf16[80,2048]{1,0:T(8,128)(2,1)S(1)}, u32[]{:S(2)}, u32[]{:S(2)}) collective-permute-start(bf16[80,2048]{1,0:T(8,128)(2,1)S(1)} %concatenate.90), channel_id=1, source_target_pairs={{0,4},{1,5},{2,6},{3,7},{4,0},{5,1},{6,2},{7,3},{8,12},{9,13},{10,... | collective-permute-start | bytes 983048 | tf_op jit(solution)/shard_map/ppermute | solution.py:10
  113.5 15.7 %collective-permute-start.22 = (bf16[80,2048]{1,0:T(8,128)(2,1)S(1)}, bf16[80,2048]{1,0:T(8,128)(2,1)S(1)}, u32[]{:S(2)}, u32[]{:S(2)}) collective-permute-start(bf16[80,2048]{1,0:T(8,128)(2,1)S(1)} %pad_maximum_fusion.8), channel_id=1, source_target_pairs={{0,2},{1,3},{2,0},{3,1},{4,6},{5,7},{6,4},{7,5},{8,10},{9,11},{10,... | collective-permute-start | bytes 983048 | tf_op jit(solution)/shard_map/ppermute | solution.py:10
  115.1 12.6 %collective-permute-start.7 = (bf16[80,2048]{1,0:T(8,128)(2,1)S(1)}, bf16[80,2048]{1,0:T(8,128)(2,1)S(1)}, u32[]{:S(2)}, u32[]{:S(2)}) collective-permute-start(bf16[80,2048]{1,0:T(8,128)(2,1)S(1)} %concatenate.89), channel_id=1, source_target_pairs={{0,4},{1,5},{2,6},{3,7},{4,0},{5,1},{6,2},{7,3},{8,12},{9,13},{10,... | collective-permute-start | bytes 983048 | tf_op jit(solution)/shard_map/ppermute | solution.py:10
  115.6 19.8 %collective-permute-start.9 = (bf16[80,2048]{1,0:T(8,128)(2,1)S(1)}, bf16[80,2048]{1,0:T(8,128)(2,1)S(1)}, u32[]{:S(2)}, u32[]{:S(2)}) collective-permute-start(bf16[80,2048]{1,0:T(8,128)(2,1)S(1)} %pad_maximum_fusion.5), channel_id=1, source_target_pairs={{0,2},{1,3},{2,0},{3,1},{4,6},{5,7},{6,4},{7,5},{8,10},{9,11},{10,... | collective-permute-start | bytes 983048 | tf_op jit(solution)/shard_map/ppermute | solution.py:10
  121.2 13.6 %collective-permute-start.21 = (bf16[40,2048]{1,0:T(8,128)(2,1)S(1)}, bf16[40,2048]{1,0:T(8,128)(2,1)S(1)}, u32[]{:S(2)}, u32[]{:S(2)}) collective-permute-start(bf16[40,2048]{1,0:T(8,128)(2,1)S(1)} %add_convert_fusion.6), channel_id=1, source_target_pairs={{0,2},{1,3},{2,0},{3,1},{4,6},{5,7},{6,4},{7,5},{8,10},{9,11},{10,... | collective-permute-start | bytes 491528 | tf_op jit(solution)/shard_map/ppermute | solution.py:10
  127.7 9.7 %collective-permute-start.8 = (bf16[40,2048]{1,0:T(8,128)(2,1)S(1)}, bf16[40,2048]{1,0:T(8,128)(2,1)S(1)}, u32[]{:S(2)}, u32[]{:S(2)}) collective-permute-start(bf16[40,2048]{1,0:T(8,128)(2,1)S(1)} %add_convert_fusion.12), channel_id=1, source_target_pairs={{0,2},{1,3},{2,0},{3,1},{4,6},{5,7},{6,4},{7,5},{8,10},{9,11},{10,... | collective-permute-start | bytes 491528 | tf_op jit(solution)/shard_map/ppermute | solution.py:10
  137.5 10.8 %collective-permute-start.10 = (bf16[40,2048]{1,0:T(8,128)(2,1)S(1)}, bf16[40,2048]{1,0:T(8,128)(2,1)S(1)}, u32[]{:S(2)}, u32[]{:S(2)}) collective-permute-start(bf16[40,2048]{1,0:T(8,128)(2,1)S(1)} %get-tuple-element.12), channel_id=1, source_target_pairs={{0,4},{1,5},{2,6},{3,7},{4,0},{5,1},{6,2},{7,3},{8,12},{9,13},{10,... | collective-permute-start | bytes 491528 | tf_op jit(solution)/shard_map/ppermute | solution.py:10
  141.1 12.3 %collective-permute-start.25 = (bf16[20,4096]{1,0:T(8,128)(2,1)S(1)}, bf16[20,4096]{1,0:T(8,128)(2,1)S(1)}, u32[]{:S(2)}, u32[]{:S(2)}) collective-permute-start(bf16[20,4096]{1,0:T(8,128)(2,1)S(1)} %get-tuple-element.32), channel_id=1, source_target_pairs={{0,8},{8,16},{16,24},{24,0},{1,9},{9,17},{17,25},{25,1},{2,10},{10... | collective-permute-start | bytes 491528 | tf_op jit(solution)/shard_map/ppermute | solution.py:14
  148.3 10.9 %collective-permute-start.24 = (bf16[20,4096]{1,0:T(8,128)(2,1)S(1)}, bf16[20,4096]{1,0:T(8,128)(2,1)S(1)}, u32[]{:S(2)}, u32[]{:S(2)}) collective-permute-start(bf16[20,4096]{1,0:T(8,128)(2,1)S(1)} %get-tuple-element.31), channel_id=1, source_target_pairs={{0,16},{8,24},{16,0},{24,8},{1,17},{9,25},{17,1},{25,9},{2,18},{10... | collective-permute-start | bytes 491528 | tf_op jit(solution)/shard_map/ppermute | solution.py:14
  148.5 11.9 %collective-permute-start.11 = (bf16[20,4096]{1,0:T(8,128)(2,1)S(1)}, bf16[20,4096]{1,0:T(8,128)(2,1)S(1)}, u32[]{:S(2)}, u32[]{:S(2)}) collective-permute-start(bf16[20,4096]{1,0:T(8,128)(2,1)S(1)} %get-tuple-element.28), channel_id=1, source_target_pairs={{0,24},{8,0},{16,8},{24,16},{1,25},{9,1},{17,9},{25,17},{2,26},{10... | collective-permute-start | bytes 491528 | tf_op jit(solution)/shard_map/ppermute | solution.py:14
  (10 other events, 128.5 us)
